TPU v7x, 512 devices: a whole 4x8x8 slice. The times are simulated.
512 devices in a mesh: req: 128 (over y, z, core), tp: 4 (over x).
Axes of the slice: x: 4, y: 8, z: 8, core: 2. Of those that a mesh axis runs over, the one named last changes fastest.
Arguments:
- tokens: bfloat16 [16384, 1024], P('req'), may hold values from -6 to 6
- attn_heads: bfloat16 [16384, 1024], P('req', 'tp'), may hold values from -6 to 6
- out_proj: bfloat16 [1024, 1024], P('tp'), may hold values from -0.1875 to 0.1875
- norm_gain: float32 [1024], replicated, may hold values from 0.3 to 1.7
- w_gate: bfloat16 [32, 1024, 512], P(None, 'req', 'tp'), may hold values from -0.1875 to 0.1875
- w_up: bfloat16 [32, 1024, 512], P(None, 'req', 'tp'), may hold values from -0.1875 to 0.1875
- w_down: bfloat16 [32, 1024, 512], P(None, 'req', 'tp'), may hold values from -0.25 to 0.25
- routes: int32 [16384, 8], P('req'), may hold values from 0 to 31, all different within a row; in each aligned block of 32 rows (0 to 31, 32 to 63, ...) at most 12 rows name the same one
- gate_weights: float32 [16384, 8], P('req'), may hold values from 0.05 to 0.45
- cache_pages: bfloat16 [1024, 128, 8, 128], P('req', None, 'tp'), may hold values from -6 to 6
- page_dest: int32 [1024], P('req'), may hold values from 0 to 1023, as said below
Outputs:
- layer_output: bfloat16 [16384, 1024], P('req', 'tp')
- decode_cache: bfloat16 [1024, 128, 8, 128], P('req', None, 'tp')
Inputs may be any that keep to these rules, and one draw needn't show every extreme that they name: `routes`: within each aligned block of 32 rows no expert is named by more than 12 rows, and some block reaches 12. The page p of index r of req (p among its 8 pages) is sent to the index r + k modulo 128 for some k from 0 to 7, into its decode slot k: page_dest[p] = ((r + k) % 128) * 8 + k. The 8 pages of one index use each k once, so every decode slot gets one page.
All inputs are finite; a program needn't handle non-finite values.
Results may differ from a plain program's by a relative error of at most 0.012.
Values may be sent and summed in bfloat16 or wider, within the bound.
A program may use at most 64 MiB of HBM per device.

v0:
```python
import jax
import jax.numpy as jnp
import numpy as np
from jax import lax
from jax.sharding import PartitionSpec as P


def passed_along(value, axis, steps):
    count = lax.axis_size(axis)
    pairs = [(source, (source + steps) % count) for source in range(count)]
    return lax.ppermute(value, axis, pairs)


def on_device(
    tokens,
    attn_heads,
    out_proj,
    norm_gain,
    w_gate,
    w_up,
    w_down,
    routes,
    gate_weights,
    cache_pages,
    page_dest,
):
    req_count = lax.axis_size("req")
    tp_count = lax.axis_size("tp")
    tp_place = lax.axis_index("tp")
    tok_count, top_count = routes.shape
    experts = w_gate.shape[0]
    model_width = tokens.shape[1]
    quarter_width = model_width // tp_count
    partial_value = jnp.dot(attn_heads, out_proj, preferred_element_type=jnp.float32)
    attention = lax.psum(partial_value.astype(jnp.bfloat16), "tp").astype(jnp.float32)
    residual = tokens.astype(jnp.float32) + attention
    inverse = lax.rsqrt(jnp.mean(residual * residual, axis=1, keepdims=True) + 1e-05)
    normed = (residual * inverse * norm_gain).astype(jnp.bfloat16)
    resid_part = lax.dynamic_slice_in_dim(residual, tp_place * quarter_width, quarter_width, 1)
    local_experts = max(1, experts // req_count)
    expert_groups = experts // local_experts
    replicas = req_count // expert_groups
    block_rows = tok_count // replicas
    capacity = 3 * block_rows * top_count // (2 * experts)
    slot_total = req_count * local_experts * capacity
    expert_ids = jnp.arange(experts, dtype=jnp.int32)
    token_hits = jnp.sum((routes[:, :, None] == expert_ids).astype(jnp.int32), axis=1)
    blocked = token_hits.reshape(replicas, block_rows, experts)
    earlier = (jnp.cumsum(blocked, axis=1) - blocked).reshape(tok_count, experts)
    slot_rank = jnp.take_along_axis(earlier, routes, axis=1)
    row_ids = jnp.arange(tok_count, dtype=jnp.int32)[:, None]
    target = row_ids // block_rows * expert_groups + routes // local_experts
    slot_ids = (target * local_experts + routes % local_experts) * capacity + slot_rank
    flat_slots = slot_ids.reshape(-1)
    flat_rows = jnp.broadcast_to(row_ids, slot_ids.shape).reshape(-1)
    slot_token = jnp.zeros((slot_total,), jnp.int32).at[flat_slots].set(flat_rows)
    slot_live = jnp.zeros((slot_total,), jnp.bfloat16).at[flat_slots].set(1.0)
    owner_table = (
        np.arange(req_count)[:, None] % expert_groups * local_experts
        + np.arange(local_experts)[None, :]
    )
    outgoing = (w_gate[owner_table], w_up[owner_table], w_down[owner_table])
    gate_full, up_full, down_full = (
        lax.all_to_all(outgoing[0], "req", split_axis=0, concat_axis=2, tiled=True),
        lax.all_to_all(outgoing[1], "req", split_axis=0, concat_axis=2, tiled=True),
        lax.all_to_all(outgoing[2], "req", split_axis=0, concat_axis=2, tiled=True),
    )
    gate_full = gate_full[0]
    up_full = up_full[0]
    down_full = down_full[0]
    outbox = (normed[slot_token] * slot_live[:, None]).reshape(
        req_count, local_experts, capacity, model_width
    )
    arrived = lax.all_to_all(outbox, "req", split_axis=0, concat_axis=0, tiled=True)
    pre_gate = jnp.einsum("recd,edh->rech", arrived, gate_full, preferred_element_type=jnp.float32)
    pre_up = jnp.einsum("recd,edh->rech", arrived, up_full, preferred_element_type=jnp.float32)
    active = (jax.nn.silu(pre_gate) * pre_up).astype(jnp.bfloat16)
    pieces = jnp.einsum(
        "rech,edh->recd", active, down_full, preferred_element_type=jnp.float32
    ).astype(jnp.bfloat16)
    returned = lax.all_to_all(pieces, "req", split_axis=0, concat_axis=0, tiled=True)
    gathered = returned.reshape(slot_total, model_width)[slot_ids]
    combined = jnp.sum(gate_weights[:, :, None] * gathered.astype(jnp.float32), axis=1)
    mixture = lax.psum_scatter(
        combined.astype(jnp.bfloat16), "tp", scatter_dimension=1, tiled=True
    ).astype(jnp.float32)
    layer_output = (resid_part + mixture).astype(jnp.bfloat16)
    spread = cache_pages.shape[0]
    page_offsets = page_dest % spread
    page_order = (
        jnp.zeros((spread,), jnp.int32).at[page_offsets].set(jnp.arange(spread, dtype=jnp.int32))
    )
    ranked = cache_pages[page_order]
    arrived_pages = [ranked[0]]
    for offset in range(1, spread):
        arrived_pages.append(passed_along(ranked[offset], "req", offset))
    decode_cache = jnp.stack(arrived_pages)
    return (layer_output, decode_cache)


def solution(mesh):
    in_specs = (
        P("req", None),
        P("req", "tp"),
        P("tp", None),
        P(),
        P(None, "req", "tp"),
        P(None, "req", "tp"),
        P(None, "req", "tp"),
        P("req", None),
        P("req", None),
        P("req", None, "tp", None),
        P("req"),
    )
    out_specs = (P("req", "tp"), P("req", None, "tp", None))
    return jax.shard_map(
        on_device, mesh=mesh, in_specs=in_specs, out_specs=out_specs, check_vma=False
    )
```

profile of v0, /device:TPU:8, one launch (start us, length us, event | category | flops | bytes accessed | tf_op | source)
XLA Modules:
  0.0 437.8 jit_solution(17030307056659740838)
XLA Ops:
  7.2 2.1 convolution_convert_fusion
  9.3 0.7 compare_select_fusion.5
  10.0 0.6 scatter_custom_fusion.2
  10.6 0.7 pad_clamp_fusion.1
  11.3 2.2 gather_fusion.1
  13.5 17.4 %all-to-all-start.1 = ((bf16[128,1,8,128]{3,2,1,0:T(8,128)(2,1)}), bf16[128,1,8,128]{3,2,1,0:T(8,128)(2,1)S(1)}, u32[]{:S(2)}, u32[]{:S(2)}) async-start(bf16[128,1,8,128]{3,2,1,0:T(8,128)(2,1)} %bitcast.3), calls=%async_computation.1 | async-start | bytes 524288 | tf_op jit(solution)/shard_map/all_to_all | solution.py:64
  30.9 0.7 convert_reduce_fusion
  31.6 0.7 bitcast_or_fusion
  32.7 7.1 %gather_fusion.6 = s32[1024]{0:T(1024)S(1)} fusion(s32[128,32]{1,0:T(8,128)S(1)} %bitcast_subtract_fusion, s32[1024]{0:T(1024)S(1)} %reshape.217), kind=kCustom, calls=%fused_computation.6 | custom fusion | bytes 16384 | tf_op jit(solution)/shard_map/jit(take_along_axis)/gather | solution.py:50
  40.3 4.3 scatter_custom_fusion
  44.6 7.6 %scatter_custom_fusion.1 = bf16[1536]{0:T(1024)(128)(2,1)S(1)} fusion(s32[1024]{0:T(1024)S(1)} %bitcast.105, bf16[1024]{0:T(1024)(128)(2,1)S(1)} %broadcast.148, bf16[]{:T(256)} %constant.106.clone.1), kind=kCustom, calls=%fused_computation.73 | custom fusion | bytes 3074 | tf_op jit(solution)/shard_map/scatter | solution.py:57
  52.4 1.4 gather_fusion.3
  53.7 14.2 %all-reduce.2.cloned.1.call-done = bf16[128,1024]{1,0:T(8,128)(2,1)} async-done(((bf16[128,1024]{1,0:T(8,128)(2,1)}), bf16[128,1024]{1,0:T(8,128)(2,1)}) %all-reduce.2.cloned.1.call-update) | async-done | bytes 262160 | tf_op jit(solution)/shard_map/psum | solution.py:35
  67.9 1.1 convert_add_fusion
  69.0 14.2 %all-to-all-start.3 = ((bf16[128,1,8,128]{3,2,1,0:T(8,128)(2,1)}), bf16[128,1,8,128]{3,2,1,0:T(8,128)(2,1)S(1)}, u32[]{:S(2)}, u32[]{:S(2)}) async-start(bf16[128,1,8,128]{3,2,1,0:T(8,128)(2,1)} %bitcast.15), calls=%async_computation.3 | async-start | bytes 524288 | tf_op jit(solution)/shard_map/all_to_all | solution.py:65
  83.2 1.1 multiply_convert_fusion
  84.3 5.8 %gather_fusion.2 = bf16[1536,1024]{1,0:T(8,128)(2,1)} fusion(bf16[128,1024]{1,0:T(8,128)(2,1)S(1)} %multiply_convert_fusion, s32[2048]{0:T(1024)S(1)} %pad_clamp_fusion), kind=kCustom, calls=%fused_computation.2 | custom fusion | bytes 6297600 | tf_op jit(solution)/shard_map/gather | solution.py:71
  90.1 6.1 %gather.28 = bf16[128,1,12,1024]{3,2,0,1:T(8,128)(2,1)} reshape(bf16[1536,1024]{1,0:T(8,128)(2,1)} %gather_fusion.2) | data formatting | bytes 6291456 | tf_op jit(solution)/shard_map/gather | solution.py:71
  96.1 4.5 %multiply_bitcast_fusion = bf16[128,1,12,1024]{3,2,1,0:T(8,128)(2,1)} fusion(bf16[128,1,12,1024]{3,2,0,1:T(8,128)(2,1)} %gather.28, bf16[128,12]{1,0:T(8,128)(2,1)S(1)} %mul.78), kind=kLoop, calls=%fused_computation.12 | loop fusion | flops 1572864 | bytes 6294528 | tf_op jit(solution)/shard_map/mul | solution.py:71
  100.6 14.3 %all-to-all-start.2 = ((bf16[128,1,12,1024]{3,2,1,0:T(8,128)(2,1)}), bf16[128,1,12,1024]{3,2,1,0:T(8,128)(2,1)}, u32[]{:S(2)}, u32[]{:S(2)}) async-start(bf16[128,1,12,1024]{3,2,1,0:T(8,128)(2,1)} %multiply_bitcast_fusion), calls=%async_computation.2 | async-start | bytes 8388608 | tf_op jit(solution)/shard_map/all_to_all | solution.py:74
  115.0 1.4 gather_fusion
  116.3 95.0 %all-to-all-done.2 = bf16[128,1,12,1024]{3,2,1,0:T(8,128)(2,1)} async-done(((bf16[128,1,12,1024]{3,2,1,0:T(8,128)(2,1)}), bf16[128,1,12,1024]{3,2,1,0:T(8,128)(2,1)}, u32[]{:S(2)}, u32[]{:S(2)}) %all-to-all-start.2) | async-done | bytes 3145760 | tf_op jit(solution)/shard_map/all_to_all | solution.py:74
  211.3 16.5 %all-to-all-start = ((bf16[128,1,8,128]{3,2,1,0:T(8,128)(2,1)}), bf16[128,1,8,128]{3,2,1,0:T(8,128)(2,1)S(1)}, u32[]{:S(2)}, u32[]{:S(2)}) async-start(bf16[128,1,8,128]{3,2,1,0:T(8,128)(2,1)} %bitcast), calls=%async_computation | async-start | bytes 524288 | tf_op jit(solution)/shard_map/all_to_all | solution.py:66
  227.8 5.8 %fusion.7 = f32[128,1,12,128]{0,3,2,1:T(8,128)S(1)} fusion(bf16[128,1,12,1024]{3,2,1,0:T(8,128)(2,1)} %all-to-all-done.2, bf16[128,1,8,128]{3,2,1,0:T(8,128)(2,1)S(1)} %all-to-all-done.1), kind=kOutput, calls=%fused_computation.20 | convolution fusion | flops 402653184 | bytes 4194304 | tf_op jit(solution)/shard_map/recd,edh->rech/dot_general | solution.py:75
  233.6 8.9 %all-to-all-done = bf16[128,1,8,128]{3,2,1,0:T(8,128)(2,1)S(1)} async-done(((bf16[128,1,8,128]{3,2,1,0:T(8,128)(2,1)}), bf16[128,1,8,128]{3,2,1,0:T(8,128)(2,1)S(1)}, u32[]{:S(2)}, u32[]{:S(2)}) %all-to-all-start) | async-done | bytes 262176 | tf_op jit(solution)/shard_map/all_to_all | solution.py:66
  242.5 8.4 %convert_bitcast_fusion = bf16[128,1,12,1024]{0,3,2,1:T(8,128)(2,1)} fusion(bf16[128,1,12,1024]{3,2,1,0:T(8,128)(2,1)} %all-to-all-done.2, f32[128,1,12,128]{0,3,2,1:T(8,128)S(1)} %fusion.7, bf16[128,1,8,128]{3,2,1,0:T(8,128)(2,1)S(1)} %all-to-all-done.3, bf16[128,1,8,128]{3,2,1,0:T(8,128)(2,1)S(1)} %all-to-all-done), kind=kOutput, calls=%fused_computation.17 | convolution fusion | flops 808058880 | bytes 7602176 | tf_op jit(solution)/shard_map/rech,edh->recd/dot_general | solution.py:78
  250.9 6.5 %copy.82 = bf16[128,1,12,1024]{3,2,1,0:T(8,128)(2,1)} copy(bf16[128,1,12,1024]{0,3,2,1:T(8,128)(2,1)} %convert_bitcast_fusion) | data formatting | bytes 6291456 | tf_op jit(solution)/shard_map/convert_element_type | solution.py:80
  257.4 7.8 %all-to-all-start.4 = ((bf16[128,1,12,1024]{3,2,1,0:T(8,128)(2,1)}), bf16[128,1,12,1024]{3,2,1,0:T(8,128)(2,1)}, u32[]{:S(2)}, u32[]{:S(2)}) async-start(bf16[128,1,12,1024]{3,2,1,0:T(8,128)(2,1)} %copy.82), calls=%async_computation.4 | async-start | bytes 8388608 | tf_op jit(solution)/shard_map/all_to_all | solution.py:81
  265.2 0.3 reduce-scatter.2.cloned.1.call-start
  265.5 1.6 gather_fusion.5
  267.1 0.4 slice_bitcast_fusion
  267.5 2.1 collective-permute-start
  269.6 3.4 collective-permute-start.1
  272.9 4.2 collective-permute-start.2
  277.1 4.6 %collective-permute-start.3 = (bf16[128,2,128]{2,1,0:T(2,128)(2,1)S(1)}, bf16[128,2,128]{2,1,0:T(2,128)(2,1)S(1)}, u32[]{:S(2)}, u32[]{:S(2)}) collective-permute-start(bf16[128,2,128]{2,1,0:T(2,128)(2,1)S(1)} %get-tuple-element.7), channel_id=1, source_target_pairs={{0,16},{4,20},{8,24},{12,28},{16,32},{20,36},{24,40},{28,44},{32,4... | collective-permute-start | bytes 196616 | tf_op jit(solution)/shard_map/ppermute | solution.py:11
  281.7 2.1 collective-permute-start.4
  284.1 74.4 %collective-permute-done = bf16[128,2,128]{2,1,0:T(2,128)(2,1)S(1)} collective-permute-done((bf16[128,2,128]{2,1,0:T(2,128)(2,1)S(1)}, bf16[128,2,128]{2,1,0:T(2,128)(2,1)S(1)}, u32[]{:S(2)}, u32[]{:S(2)}) %collective-permute-start) | collective-permute-done | bytes 65568 | tf_op jit(solution)/shard_map/ppermute | solution.py:11
  358.5 5.6 %collective-permute-start.5 = (bf16[128,2,128]{2,1,0:T(2,128)(2,1)S(1)}, bf16[128,2,128]{2,1,0:T(2,128)(2,1)S(1)}, u32[]{:S(2)}, u32[]{:S(2)}) collective-permute-start(bf16[128,2,128]{2,1,0:T(2,128)(2,1)S(1)} %get-tuple-element.5), channel_id=1, source_target_pairs={{0,24},{4,28},{8,32},{12,36},{16,40},{20,44},{24,48},{28,52},{32,5... | collective-permute-start | bytes 196616 | tf_op jit(solution)/shard_map/ppermute | solution.py:11
  364.2 22.5 %collective-permute-start.6 = (bf16[128,2,128]{2,1,0:T(2,128)(2,1)S(1)}, bf16[128,2,128]{2,1,0:T(2,128)(2,1)}, u32[]{:S(2)}, u32[]{:S(2)}) collective-permute-start(bf16[128,2,128]{2,1,0:T(2,128)(2,1)S(1)} %get-tuple-element.4), channel_id=1, source_target_pairs={{0,28},{4,32},{8,36},{12,40},{16,44},{20,48},{24,52},{28,56},{32,6... | collective-permute-start | bytes 196616 | tf_op jit(solution)/shard_map/ppermute | solution.py:11
  386.9 0.8 copy-done.5
  387.7 6.1 %reshape.168 = bf16[1536,1024]{1,0:T(8,128)(2,1)} reshape(bf16[128,1,12,1024]{3,2,1,0:T(8,128)(2,1)} %all-to-all-done.4) | data formatting | bytes 6291456 | tf_op jit(solution)/shard_map/reshape | solution.py:82
  393.8 7.3 %gather_fusion.4 = bf16[1024,1024]{1,0:T(8,128)(2,1)S(1)} fusion(bf16[1536,1024]{1,0:T(8,128)(2,1)} %reshape.168, s32[1024]{0:T(1024)S(1)} %broadcast_clamp_fusion), kind=kCustom, calls=%fused_computation.4 | custom fusion | bytes 4198400 | tf_op jit(solution)/shard_map/gather | solution.py:82
  401.1 2.0 fusion
  403.1 0.7 bitcast_dynamic-update-slice_fusion.2
  403.8 0.7 bitcast_dynamic-update-slice_fusion.1
  404.5 1.5 bitcast_dynamic-update-slice_fusion
  406.0 23.4 %reduce-scatter.2.cloned.1.call-done = bf16[128,256]{1,0:T(8,128)(2,1)} async-done(((bf16[128,1024]{1,0:T(8,128)(2,1)}), bf16[128,256]{1,0:T(8,128)(2,1)}) %reduce-scatter.2.cloned.1.call-update) | async-done | bytes 65552 | tf_op jit(solution)/shard_map/reduce_scatter | solution.py:84
  429.5 1.5 add_convert_fusion
  (56 shorter events, 1.7 us)
Async XLA Ops:
  7.2 258.3 %copy-start = (bf16[8,128,2,128]{3,2,1,0:T(2,128)(2,1)S(1)}, bf16[8,128,2,128]{3,2,1,0:T(2,128)(2,1)}, u32[]{:S(2)}) copy-start(bf16[8,128,2,128]{3,2,1,0:T(2,128)(2,1)} %param.24) | copy-start | bytes 1572868
  7.2 60.7 %all-reduce.2.cloned.1.call-start = ((), (), s32[]{:S(2)}) async-start(), calls=%async_computation.6 | async-start | bytes 524288 | tf_op jit(solution)/shard_map/psum | solution.py:35
  13.5 55.5 %all-to-all-start.1 = ((bf16[128,1,8,128]{3,2,1,0:T(8,128)(2,1)}), bf16[128,1,8,128]{3,2,1,0:T(8,128)(2,1)S(1)}, u32[]{:S(2)}, u32[]{:S(2)}) async-start(bf16[128,1,8,128]{3,2,1,0:T(8,128)(2,1)} %bitcast.3), calls=%async_computation.1 | async-start | bytes 524288 | tf_op jit(solution)/shard_map/all_to_all | solution.py:64
  32.6 7.3 %copy-start.4 = (s32[128,8]{0,1:T(8,128)S(1)}, s32[128,8]{0,1:T(8,128)}, u32[]{:S(2)}) copy-start(s32[128,8]{0,1:T(8,128)} %param.22) | copy-start | bytes 12292
  32.7 19.7 %copy-start.1 = (bf16[32,8,128]{2,1,0:T(8,128)(2,1)S(1)}, bf16[32,8,128]{2,1,0:T(8,128)(2,1)}, u32[]{:S(2)}) copy-start(bf16[32,8,128]{2,1,0:T(8,128)(2,1)} %param.20) | copy-start | bytes 196612
  32.7 35.2 %copy-start.3 = (bf16[128,1024]{1,0:T(8,128)(2,1)S(1)}, bf16[128,1024]{1,0:T(8,128)(2,1)}, u32[]{:S(2)}) copy-start(bf16[128,1024]{1,0:T(8,128)(2,1)} %param.15) | copy-start | bytes 786436
  32.7 50.5 %copy-start.6 = (f32[1024]{0:T(1024)S(1)}, f32[1024]{0:T(1024)}, u32[]{:S(2)}) copy-start(f32[1024]{0:T(1024)} %param.18) | copy-start | bytes 12292
  69.0 31.6 %all-to-all-start.3 = ((bf16[128,1,8,128]{3,2,1,0:T(8,128)(2,1)}), bf16[128,1,8,128]{3,2,1,0:T(8,128)(2,1)S(1)}, u32[]{:S(2)}, u32[]{:S(2)}) async-start(bf16[128,1,8,128]{3,2,1,0:T(8,128)(2,1)} %bitcast.15), calls=%async_computation.3 | async-start | bytes 524288 | tf_op jit(solution)/shard_map/all_to_all | solution.py:65
  100.6 14.3 %copy-start.2 = (bf16[32,8,128]{2,1,0:T(8,128)(2,1)S(1)}, bf16[32,8,128]{2,1,0:T(8,128)(2,1)}, u32[]{:S(2)}) copy-start(bf16[32,8,128]{2,1,0:T(8,128)(2,1)} %param.21) | copy-start | bytes 196612
  100.6 110.7 %all-to-all-start.2 = ((bf16[128,1,12,1024]{3,2,1,0:T(8,128)(2,1)}), bf16[128,1,12,1024]{3,2,1,0:T(8,128)(2,1)}, u32[]{:S(2)}, u32[]{:S(2)}) async-start(bf16[128,1,12,1024]{3,2,1,0:T(8,128)(2,1)} %multiply_bitcast_fusion), calls=%async_computation.2 | async-start | bytes 8388608 | tf_op jit(solution)/shard_map/all_to_all | solution.py:74
  211.3 31.2 %all-to-all-start = ((bf16[128,1,8,128]{3,2,1,0:T(8,128)(2,1)}), bf16[128,1,8,128]{3,2,1,0:T(8,128)(2,1)S(1)}, u32[]{:S(2)}, u32[]{:S(2)}) async-start(bf16[128,1,8,128]{3,2,1,0:T(8,128)(2,1)} %bitcast), calls=%async_computation | async-start | bytes 524288 | tf_op jit(solution)/shard_map/all_to_all | solution.py:66
  257.4 26.6 %copy-start.7 = (f32[128,8]{0,1:T(8,128)S(1)}, f32[128,8]{0,1:T(8,128)}, u32[]{:S(2)}) copy-start(f32[128,8]{0,1:T(8,128)} %param.23) | copy-start | bytes 12292
  257.4 129.5 %all-to-all-start.4 = ((bf16[128,1,12,1024]{3,2,1,0:T(8,128)(2,1)}), bf16[128,1,12,1024]{3,2,1,0:T(8,128)(2,1)}, u32[]{:S(2)}, u32[]{:S(2)}) async-start(bf16[128,1,12,1024]{3,2,1,0:T(8,128)(2,1)} %copy.82), calls=%async_computation.4 | async-start | bytes 8388608 | tf_op jit(solution)/shard_map/all_to_all | solution.py:81
  265.2 164.2 %reduce-scatter.2.cloned.1.call-start = ((), (), s32[]{:S(2)}) async-start(), calls=%async_computation.7 | async-start | bytes 327680 | tf_op jit(solution)/shard_map/reduce_scatter | solution.py:84
  267.5 91.0 %collective-permute-start = (bf16[128,2,128]{2,1,0:T(2,128)(2,1)S(1)}, bf16[128,2,128]{2,1,0:T(2,128)(2,1)S(1)}, u32[]{:S(2)}, u32[]{:S(2)}) collective-permute-start(bf16[128,2,128]{2,1,0:T(2,128)(2,1)S(1)} %get-tuple-element.10), channel_id=1, source_target_pairs={{0,4},{4,8},{8,12},{12,16},{16,20},{20,24},{24,28},{28,32},{32,36}... | collective-permute-start | bytes 196616 | tf_op jit(solution)/shard_map/ppermute | solution.py:11
  269.6 94.6 %collective-permute-start.1 = (bf16[128,2,128]{2,1,0:T(2,128)(2,1)S(1)}, bf16[128,2,128]{2,1,0:T(2,128)(2,1)S(1)}, u32[]{:S(2)}, u32[]{:S(2)}) collective-permute-start(bf16[128,2,128]{2,1,0:T(2,128)(2,1)S(1)} %get-tuple-element.9), channel_id=1, source_target_pairs={{0,8},{4,12},{8,16},{12,20},{16,24},{20,28},{24,32},{28,36},{32,40... | collective-permute-start | bytes 196616 | tf_op jit(solution)/shard_map/ppermute | solution.py:11
  272.9 113.8 %collective-permute-start.2 = (bf16[128,2,128]{2,1,0:T(2,128)(2,1)S(1)}, bf16[128,2,128]{2,1,0:T(2,128)(2,1)S(1)}, u32[]{:S(2)}, u32[]{:S(2)}) collective-permute-start(bf16[128,2,128]{2,1,0:T(2,128)(2,1)S(1)} %get-tuple-element.8), channel_id=1, source_target_pairs={{0,12},{4,16},{8,20},{12,24},{16,28},{20,32},{24,36},{28,40},{32,4... | collective-permute-start | bytes 196616 | tf_op jit(solution)/shard_map/ppermute | solution.py:11
  277.1 109.7 %collective-permute-start.3 = (bf16[128,2,128]{2,1,0:T(2,128)(2,1)S(1)}, bf16[128,2,128]{2,1,0:T(2,128)(2,1)S(1)}, u32[]{:S(2)}, u32[]{:S(2)}) collective-permute-start(bf16[128,2,128]{2,1,0:T(2,128)(2,1)S(1)} %get-tuple-element.7), channel_id=1, source_target_pairs={{0,16},{4,20},{8,24},{12,28},{16,32},{20,36},{24,40},{28,44},{32,4... | collective-permute-start | bytes 196616 | tf_op jit(solution)/shard_map/ppermute | solution.py:11
  281.7 121.4 %collective-permute-start.4 = (bf16[128,2,128]{2,1,0:T(2,128)(2,1)S(1)}, bf16[128,2,128]{2,1,0:T(2,128)(2,1)S(1)}, u32[]{:S(2)}, u32[]{:S(2)}) collective-permute-start(bf16[128,2,128]{2,1,0:T(2,128)(2,1)S(1)} %get-tuple-element.6), channel_id=1, source_target_pairs={{0,20},{4,24},{8,28},{12,32},{16,36},{20,40},{24,44},{28,48},{32,5... | collective-permute-start | bytes 196616 | tf_op jit(solution)/shard_map/ppermute | solution.py:11
  358.5 45.3 %collective-permute-start.5 = (bf16[128,2,128]{2,1,0:T(2,128)(2,1)S(1)}, bf16[128,2,128]{2,1,0:T(2,128)(2,1)S(1)}, u32[]{:S(2)}, u32[]{:S(2)}) collective-permute-start(bf16[128,2,128]{2,1,0:T(2,128)(2,1)S(1)} %get-tuple-element.5), channel_id=1, source_target_pairs={{0,24},{4,28},{8,32},{12,36},{16,40},{20,44},{24,48},{28,52},{32,5... | collective-permute-start | bytes 196616 | tf_op jit(solution)/shard_map/ppermute | solution.py:11
  364.2 40.3 %collective-permute-start.6 = (bf16[128,2,128]{2,1,0:T(2,128)(2,1)S(1)}, bf16[128,2,128]{2,1,0:T(2,128)(2,1)}, u32[]{:S(2)}, u32[]{:S(2)}) collective-permute-start(bf16[128,2,128]{2,1,0:T(2,128)(2,1)S(1)} %get-tuple-element.4), channel_id=1, source_target_pairs={{0,28},{4,32},{8,36},{12,40},{16,44},{20,48},{24,52},{28,56},{32,6... | collective-permute-start | bytes 196616 | tf_op jit(solution)/shard_map/ppermute | solution.py:11
  386.9 0.8 copy-start.5
Sparse Core Ops, SparseCore 0:
  10.9 56.9 all-reduce.1
  403.2 26.1 reduce-scatter.1
where the time goes:
time: 439 us; the launch traced here: 438 us
  waiting for transfers between devices  216 us (49%)
  starting transfers between devices  115 us (26%)
  local copies, waits for them, and re-layouts  63.4 us (14%)
  matrix products  16.2 us (4%)
  between operations  14.4 us (3%)
  other arithmetic  13 us (3%)
    all_to_all x1, waiting for transfers between devices, on_device(): lax.all_to_all(outbox, 'req', split_axis=0, concat_axis=0, tiled=True)  95 us
    ppermute x7, waiting for transfers between devices, passed_along(): return lax.ppermute(value, axis, pairs)  74.4 us
    ppermute x7, starting transfers between devices, passed_along(): return lax.ppermute(value, axis, pairs)  44.4 us
    reduce_scatter x1, waiting for transfers between devices, on_device(): lax.psum_scatter(combined.astype(jnp.bfloat16), 'tp', scatter_dimension=1...  23.4 us
    all_to_all x1, starting transfers between devices, on_device(): lax.all_to_all(outgoing[0], 'req', split_axis=0, concat_axis=2, tiled=True)  17.4 us
    all_to_all x1, starting transfers between devices, on_device(): lax.all_to_all(outgoing[2], 'req', split_axis=0, concat_axis=2, tiled=True)  16.5 us
    all_to_all x1, starting transfers between devices, on_device(): lax.all_to_all(outbox, 'req', split_axis=0, concat_axis=0, tiled=True)  14.3 us
    all_to_all x1, starting transfers between devices, on_device(): lax.all_to_all(outgoing[1], 'req', split_axis=0, concat_axis=2, tiled=True)  14.2 us
  transfers between devices with their start and end apart: 14, of which 5 were waited for; matrix products, arithmetic and copies ran while one was open for 17% of the time, Pallas kernels for 0%

commit v1 on v0

--- a/solution.py
+++ b/solution.py
@@ -3,6 +3,10 @@
 import numpy as np
 from jax import lax
 from jax.sharding import PartitionSpec as P
+
+
+def convert_sites(arr_in, axis_tag):
+    return lax.all_gather(arr_in, axis_tag).sum(axis=0)
 
 
 def passed_along(value, axis, steps):
@@ -32,7 +36,7 @@
     model_width = tokens.shape[1]
     quarter_width = model_width // tp_count
     partial_value = jnp.dot(attn_heads, out_proj, preferred_element_type=jnp.float32)
-    attention = lax.psum(partial_value.astype(jnp.bfloat16), "tp").astype(jnp.float32)
+    attention = convert_sites(partial_value.astype(jnp.bfloat16), "tp").astype(jnp.float32)
     residual = tokens.astype(jnp.float32) + attention
     inverse = lax.rsqrt(jnp.mean(residual * residual, axis=1, keepdims=True) + 1e-05)
     normed = (residual * inverse * norm_gain).astype(jnp.bfloat16)

time: 439 us -> 425 us (0.968)
  waiting for transfers between devices: 216 us -> 202 us
    psum x1 -> x0, waiting for transfers between devices: 14.2 us -> none  [on_device(): lax.psum(partial_value.astype(jnp.bfloat16), 'tp').astype(jnp.float32)]
  transfers between devices with their start and end apart: 14 -> 14, of which waited for: 5 -> 4; matrix products, arithmetic and copies ran while one was open for 17% -> 17% of each run, Pallas kernels for 0% -> 0%
where the time goes in v1:
time: 425 us; the launch traced here: 424 us
  waiting for transfers between devices  202 us (48%)
  starting transfers between devices  114 us (27%)
  local copies, waits for them, and re-layouts  63.4 us (15%)
  matrix products  17.3 us (4%)
  between operations  14.4 us (3%)
  other arithmetic  12.6 us (3%)
    all_to_all x1, waiting for transfers between devices, on_device(): lax.all_to_all(outbox, 'req', split_axis=0, concat_axis=0, tiled=True)  95 us
    ppermute x7, waiting for transfers between devices, passed_along(): return lax.ppermute(value, axis, pairs)  74.4 us
    ppermute x7, starting transfers between devices, passed_along(): return lax.ppermute(value, axis, pairs)  44.4 us
    reduce_scatter x1, waiting for transfers between devices, on_device(): lax.psum_scatter(combined.astype(jnp.bfloat16), 'tp', scatter_dimension=1...  24.3 us
    all_to_all x1, starting transfers between devices, on_device(): lax.all_to_all(outgoing[0], 'req', split_axis=0, concat_axis=2, tiled=True)  17.4 us
    all_to_all x1, starting transfers between devices, on_device(): lax.all_to_all(outgoing[2], 'req', split_axis=0, concat_axis=2, tiled=True)  16.5 us
    all_to_all x1, starting transfers between devices, on_device(): lax.all_to_all(outbox, 'req', split_axis=0, concat_axis=0, tiled=True)  14.3 us
    all_to_all x1, starting transfers between devices, on_device(): lax.all_to_all(outgoing[1], 'req', split_axis=0, concat_axis=2, tiled=True)  13.7 us
  transfers between devices with their start and end apart: 14, of which 4 were waited for; matrix products, arithmetic and copies ran while one was open for 17% of the time, Pallas kernels for 0%

profile of v1, /device:TPU:8, one launch (start us, length us, event | category | flops | bytes accessed | tf_op | source)
XLA Modules:
  0.0 423.8 jit_solution(14566156517347515180)
XLA Ops:
  7.2 2.1 convolution_convert_fusion
  9.3 0.7 compare_select_fusion.5
  10.0 0.6 scatter_custom_fusion.2
  10.6 0.7 pad_clamp_fusion.1
  11.3 2.2 gather_fusion.1
  13.5 17.4 %all-to-all-start.1 = ((bf16[128,1,8,128]{3,2,1,0:T(8,128)(2,1)}), bf16[128,1,8,128]{3,2,1,0:T(8,128)(2,1)S(1)}, u32[]{:S(2)}, u32[]{:S(2)}) async-start(bf16[128,1,8,128]{3,2,1,0:T(8,128)(2,1)} %bitcast.4), calls=%async_computation.1 | async-start | bytes 524288 | tf_op jit(solution)/shard_map/all_to_all | solution.py:68
  30.8 0.7 convert_reduce_fusion
  31.7 0.7 bitcast_or_fusion
  32.7 7.1 %gather_fusion.6 = s32[1024]{0:T(1024)S(1)} fusion(s32[128,32]{1,0:T(8,128)S(1)} %bitcast_subtract_fusion, s32[1024]{0:T(1024)S(1)} %reshape.217), kind=kCustom, calls=%fused_computation.6 | custom fusion | bytes 16384 | tf_op jit(solution)/shard_map/jit(take_along_axis)/gather | solution.py:54
  40.3 4.3 %scatter_custom_fusion = s32[1536]{0:T(1024)S(1)} fusion(s32[1024]{0:T(1024)S(1)} %bitcast.106, s32[1024]{0:T(1024)S(1)} %reshape.227, s32[]{:T(128)} %constant.92.clone.1), kind=kCustom, calls=%fused_computation.66 | custom fusion | bytes 6148 | tf_op jit(solution)/shard_map/scatter | solution.py:60
  44.6 7.6 %scatter_custom_fusion.1 = bf16[1536]{0:T(1024)(128)(2,1)S(1)} fusion(s32[1024]{0:T(1024)S(1)} %bitcast.107, bf16[1024]{0:T(1024)(128)(2,1)S(1)} %broadcast.148, bf16[]{:T(256)} %constant.91.clone.1), kind=kCustom, calls=%fused_computation.73 | custom fusion | bytes 3074 | tf_op jit(solution)/shard_map/scatter | solution.py:61
  52.2 0.1 mul.78
  52.4 1.4 gather_fusion.3
  53.7 1.4 reduce_sum.39
  55.2 0.2 convert_add_fusion
  55.4 13.7 %all-to-all-start.3 = ((bf16[128,1,8,128]{3,2,1,0:T(8,128)(2,1)}), bf16[128,1,8,128]{3,2,1,0:T(8,128)(2,1)S(1)}, u32[]{:S(2)}, u32[]{:S(2)}) async-start(bf16[128,1,8,128]{3,2,1,0:T(8,128)(2,1)} %bitcast.16), calls=%async_computation.3 | async-start | bytes 524288 | tf_op jit(solution)/shard_map/all_to_all | solution.py:69
  69.2 5.8 %gather_fusion.2 = bf16[1536,1024]{1,0:T(8,128)(2,1)} fusion(bf16[128,1024]{1,0:T(8,128)(2,1)S(1)} %multiply_convert_fusion, s32[2048]{0:T(1024)S(1)} %pad_clamp_fusion), kind=kCustom, calls=%fused_computation.2 | custom fusion | bytes 6297600 | tf_op jit(solution)/shard_map/gather | solution.py:75
  75.0 6.1 %gather.28 = bf16[128,1,12,1024]{3,2,0,1:T(8,128)(2,1)} reshape(bf16[1536,1024]{1,0:T(8,128)(2,1)} %gather_fusion.2) | data formatting | bytes 6291456 | tf_op jit(solution)/shard_map/gather | solution.py:75
  81.1 4.5 %multiply_bitcast_fusion = bf16[128,1,12,1024]{3,2,1,0:T(8,128)(2,1)} fusion(bf16[128,1,12,1024]{3,2,0,1:T(8,128)(2,1)} %gather.28, bf16[128,12]{1,0:T(8,128)(2,1)S(1)} %mul.78), kind=kLoop, calls=%fused_computation.12 | loop fusion | flops 1572864 | bytes 6294528 | tf_op jit(solution)/shard_map/mul | solution.py:75
  85.6 14.3 %all-to-all-start.2 = ((bf16[128,1,12,1024]{3,2,1,0:T(8,128)(2,1)}), bf16[128,1,12,1024]{3,2,1,0:T(8,128)(2,1)}, u32[]{:S(2)}, u32[]{:S(2)}) async-start(bf16[128,1,12,1024]{3,2,1,0:T(8,128)(2,1)} %multiply_bitcast_fusion), calls=%async_computation.2 | async-start | bytes 8388608 | tf_op jit(solution)/shard_map/all_to_all | solution.py:78
  99.9 1.4 gather_fusion
  101.3 95.0 %all-to-all-done.2 = bf16[128,1,12,1024]{3,2,1,0:T(8,128)(2,1)} async-done(((bf16[128,1,12,1024]{3,2,1,0:T(8,128)(2,1)}), bf16[128,1,12,1024]{3,2,1,0:T(8,128)(2,1)}, u32[]{:S(2)}, u32[]{:S(2)}) %all-to-all-start.2) | async-done | bytes 3145760 | tf_op jit(solution)/shard_map/all_to_all | solution.py:78
  196.3 16.5 %all-to-all-start = ((bf16[128,1,8,128]{3,2,1,0:T(8,128)(2,1)}), bf16[128,1,8,128]{3,2,1,0:T(8,128)(2,1)S(1)}, u32[]{:S(2)}, u32[]{:S(2)}) async-start(bf16[128,1,8,128]{3,2,1,0:T(8,128)(2,1)} %bitcast.1), calls=%async_computation | async-start | bytes 524288 | tf_op jit(solution)/shard_map/all_to_all | solution.py:70
  212.7 6.7 %fusion.7 = f32[128,1,12,128]{0,3,2,1:T(8,128)} fusion(bf16[128,1,12,1024]{3,2,1,0:T(8,128)(2,1)} %all-to-all-done.2, bf16[128,1,8,128]{3,2,1,0:T(8,128)(2,1)S(1)} %all-to-all-done.1), kind=kOutput, calls=%fused_computation.20 | convolution fusion | flops 402653184 | bytes 4194304 | tf_op jit(solution)/shard_map/recd,edh->rech/dot_general | solution.py:79
  219.4 8.1 %all-to-all-done = bf16[128,1,8,128]{3,2,1,0:T(8,128)(2,1)S(1)} async-done(((bf16[128,1,8,128]{3,2,1,0:T(8,128)(2,1)}), bf16[128,1,8,128]{3,2,1,0:T(8,128)(2,1)S(1)}, u32[]{:S(2)}, u32[]{:S(2)}) %all-to-all-start) | async-done | bytes 262176 | tf_op jit(solution)/shard_map/all_to_all | solution.py:70
  227.5 8.6 %convert_bitcast_fusion = bf16[128,1,12,1024]{0,3,2,1:T(8,128)(2,1)} fusion(bf16[128,1,12,1024]{3,2,1,0:T(8,128)(2,1)} %all-to-all-done.2, f32[128,1,12,128]{0,3,2,1:T(8,128)} %fusion.7, bf16[128,1,8,128]{3,2,1,0:T(8,128)(2,1)S(1)} %all-to-all-done.3, bf16[128,1,8,128]{3,2,1,0:T(8,128)(2,1)S(1)} %all-to-all-done), kind=kOutput, calls=%fused_computation.17 | convolution fusion | flops 808058880 | bytes 7602176 | tf_op jit(solution)/shard_map/rech,edh->recd/dot_general | solution.py:82
  236.1 6.5 %copy.82 = bf16[128,1,12,1024]{3,2,1,0:T(8,128)(2,1)} copy(bf16[128,1,12,1024]{0,3,2,1:T(8,128)(2,1)} %convert_bitcast_fusion) | data formatting | bytes 6291456 | tf_op jit(solution)/shard_map/convert_element_type | solution.py:84
  242.6 7.8 %all-to-all-start.4 = ((bf16[128,1,12,1024]{3,2,1,0:T(8,128)(2,1)}), bf16[128,1,12,1024]{3,2,1,0:T(8,128)(2,1)}, u32[]{:S(2)}, u32[]{:S(2)}) async-start(bf16[128,1,12,1024]{3,2,1,0:T(8,128)(2,1)} %copy.82), calls=%async_computation.4 | async-start | bytes 8388608 | tf_op jit(solution)/shard_map/all_to_all | solution.py:85
  250.4 0.3 reduce-scatter.2.cloned.1.call-start
  250.7 1.6 gather_fusion.5
  252.3 0.4 slice_bitcast_fusion
  252.7 2.1 collective-permute-start
  254.7 3.4 collective-permute-start.1
  258.1 4.2 collective-permute-start.2
  262.3 4.6 %collective-permute-start.3 = (bf16[128,2,128]{2,1,0:T(2,128)(2,1)S(1)}, bf16[128,2,128]{2,1,0:T(2,128)(2,1)S(1)}, u32[]{:S(2)}, u32[]{:S(2)}) collective-permute-start(bf16[128,2,128]{2,1,0:T(2,128)(2,1)S(1)} %get-tuple-element.7), channel_id=1, source_target_pairs={{0,16},{4,20},{8,24},{12,28},{16,32},{20,36},{24,40},{28,44},{32,4... | collective-permute-start | bytes 196616 | tf_op jit(solution)/shard_map/ppermute | solution.py:15
  266.9 2.1 collective-permute-start.4
  269.3 74.4 %collective-permute-done = bf16[128,2,128]{2,1,0:T(2,128)(2,1)S(1)} collective-permute-done((bf16[128,2,128]{2,1,0:T(2,128)(2,1)S(1)}, bf16[128,2,128]{2,1,0:T(2,128)(2,1)S(1)}, u32[]{:S(2)}, u32[]{:S(2)}) %collective-permute-start) | collective-permute-done | bytes 65568 | tf_op jit(solution)/shard_map/ppermute | solution.py:15
  343.7 5.6 %collective-permute-start.5 = (bf16[128,2,128]{2,1,0:T(2,128)(2,1)S(1)}, bf16[128,2,128]{2,1,0:T(2,128)(2,1)S(1)}, u32[]{:S(2)}, u32[]{:S(2)}) collective-permute-start(bf16[128,2,128]{2,1,0:T(2,128)(2,1)S(1)} %get-tuple-element.5), channel_id=1, source_target_pairs={{0,24},{4,28},{8,32},{12,36},{16,40},{20,44},{24,48},{28,52},{32,5... | collective-permute-start | bytes 196616 | tf_op jit(solution)/shard_map/ppermute | solution.py:15
  349.4 22.5 %collective-permute-start.6 = (bf16[128,2,128]{2,1,0:T(2,128)(2,1)S(1)}, bf16[128,2,128]{2,1,0:T(2,128)(2,1)}, u32[]{:S(2)}, u32[]{:S(2)}) collective-permute-start(bf16[128,2,128]{2,1,0:T(2,128)(2,1)S(1)} %get-tuple-element.4), channel_id=1, source_target_pairs={{0,28},{4,32},{8,36},{12,40},{16,44},{20,48},{24,52},{28,56},{32,6... | collective-permute-start | bytes 196616 | tf_op jit(solution)/shard_map/ppermute | solution.py:15
  372.1 0.8 copy-done.5
  372.9 6.1 %reshape.168 = bf16[1536,1024]{1,0:T(8,128)(2,1)} reshape(bf16[128,1,12,1024]{3,2,1,0:T(8,128)(2,1)} %all-to-all-done.4) | data formatting | bytes 6291456 | tf_op jit(solution)/shard_map/reshape | solution.py:86
  379.0 7.3 %gather_fusion.4 = bf16[1024,1024]{1,0:T(8,128)(2,1)S(1)} fusion(bf16[1536,1024]{1,0:T(8,128)(2,1)} %reshape.168, s32[1024]{0:T(1024)S(1)} %broadcast_clamp_fusion), kind=kCustom, calls=%fused_computation.4 | custom fusion | bytes 4198400 | tf_op jit(solution)/shard_map/gather | solution.py:86
  386.3 2.0 fusion
  388.3 0.7 bitcast_dynamic-update-slice_fusion.2
  389.0 0.7 bitcast_dynamic-update-slice_fusion.1
  389.7 1.5 bitcast_dynamic-update-slice_fusion
  391.2 24.3 %reduce-scatter.2.cloned.1.call-done = bf16[128,256]{1,0:T(8,128)(2,1)} async-done(((bf16[128,1024]{1,0:T(8,128)(2,1)}), bf16[128,256]{1,0:T(8,128)(2,1)}) %reduce-scatter.2.cloned.1.call-update) | async-done | bytes 65552 | tf_op jit(solution)/shard_map/reduce_scatter | solution.py:88
  415.5 1.5 add_convert_fusion
  (57 shorter events, 1.7 us)
Async XLA Ops:
  7.2 243.5 %copy-start = (bf16[8,128,2,128]{3,2,1,0:T(2,128)(2,1)S(1)}, bf16[8,128,2,128]{3,2,1,0:T(2,128)(2,1)}, u32[]{:S(2)}) copy-start(bf16[8,128,2,128]{3,2,1,0:T(2,128)(2,1)} %param.24) | copy-start | bytes 1572868
  7.2 46.6 %all-gather.3.cloned.1.call-start = ((), (), s32[]{:S(2)}) async-start(), calls=%async_computation.7 | async-start | bytes 1310720 | tf_op jit(solution)/shard_map/all_gather | solution.py:9
  13.5 41.9 %all-to-all-start.1 = ((bf16[128,1,8,128]{3,2,1,0:T(8,128)(2,1)}), bf16[128,1,8,128]{3,2,1,0:T(8,128)(2,1)S(1)}, u32[]{:S(2)}, u32[]{:S(2)}) async-start(bf16[128,1,8,128]{3,2,1,0:T(8,128)(2,1)} %bitcast.4), calls=%async_computation.1 | async-start | bytes 524288 | tf_op jit(solution)/shard_map/all_to_all | solution.py:68
  32.6 7.3 %copy-start.4 = (s32[128,8]{0,1:T(8,128)S(1)}, s32[128,8]{0,1:T(8,128)}, u32[]{:S(2)}) copy-start(s32[128,8]{0,1:T(8,128)} %param.22) | copy-start | bytes 12292
  32.7 19.7 %copy-start.1 = (bf16[32,8,128]{2,1,0:T(8,128)(2,1)S(1)}, bf16[32,8,128]{2,1,0:T(8,128)(2,1)}, u32[]{:S(2)}) copy-start(bf16[32,8,128]{2,1,0:T(8,128)(2,1)} %param.20) | copy-start | bytes 196612
  32.7 22.5 %copy-start.3 = (bf16[128,1024]{1,0:T(8,128)(2,1)S(1)}, bf16[128,1024]{1,0:T(8,128)(2,1)}, u32[]{:S(2)}) copy-start(bf16[128,1024]{1,0:T(8,128)(2,1)} %param.15) | copy-start | bytes 786436
  32.7 36.4 %copy-start.6 = (f32[1024]{0:T(1024)S(1)}, f32[1024]{0:T(1024)}, u32[]{:S(2)}) copy-start(f32[1024]{0:T(1024)} %param.18) | copy-start | bytes 12292
  55.4 30.2 %all-to-all-start.3 = ((bf16[128,1,8,128]{3,2,1,0:T(8,128)(2,1)}), bf16[128,1,8,128]{3,2,1,0:T(8,128)(2,1)S(1)}, u32[]{:S(2)}, u32[]{:S(2)}) async-start(bf16[128,1,8,128]{3,2,1,0:T(8,128)(2,1)} %bitcast.16), calls=%async_computation.3 | async-start | bytes 524288 | tf_op jit(solution)/shard_map/all_to_all | solution.py:69
  85.6 14.3 %copy-start.2 = (bf16[32,8,128]{2,1,0:T(8,128)(2,1)S(1)}, bf16[32,8,128]{2,1,0:T(8,128)(2,1)}, u32[]{:S(2)}) copy-start(bf16[32,8,128]{2,1,0:T(8,128)(2,1)} %param.21) | copy-start | bytes 196612
  85.6 110.7 %all-to-all-start.2 = ((bf16[128,1,12,1024]{3,2,1,0:T(8,128)(2,1)}), bf16[128,1,12,1024]{3,2,1,0:T(8,128)(2,1)}, u32[]{:S(2)}, u32[]{:S(2)}) async-start(bf16[128,1,12,1024]{3,2,1,0:T(8,128)(2,1)} %multiply_bitcast_fusion), calls=%async_computation.2 | async-start | bytes 8388608 | tf_op jit(solution)/shard_map/all_to_all | solution.py:78
  196.3 31.2 %all-to-all-start = ((bf16[128,1,8,128]{3,2,1,0:T(8,128)(2,1)}), bf16[128,1,8,128]{3,2,1,0:T(8,128)(2,1)S(1)}, u32[]{:S(2)}, u32[]{:S(2)}) async-start(bf16[128,1,8,128]{3,2,1,0:T(8,128)(2,1)} %bitcast.1), calls=%async_computation | async-start | bytes 524288 | tf_op jit(solution)/shard_map/all_to_all | solution.py:70
  242.6 26.6 %copy-start.7 = (f32[128,8]{0,1:T(8,128)S(1)}, f32[128,8]{0,1:T(8,128)}, u32[]{:S(2)}) copy-start(f32[128,8]{0,1:T(8,128)} %param.23) | copy-start | bytes 12292
  242.6 129.5 %all-to-all-start.4 = ((bf16[128,1,12,1024]{3,2,1,0:T(8,128)(2,1)}), bf16[128,1,12,1024]{3,2,1,0:T(8,128)(2,1)}, u32[]{:S(2)}, u32[]{:S(2)}) async-start(bf16[128,1,12,1024]{3,2,1,0:T(8,128)(2,1)} %copy.82), calls=%async_computation.4 | async-start | bytes 8388608 | tf_op jit(solution)/shard_map/all_to_all | solution.py:85
  250.4 165.1 %reduce-scatter.2.cloned.1.call-start = ((), (), s32[]{:S(2)}) async-start(), calls=%async_computation.6 | async-start | bytes 327680 | tf_op jit(solution)/shard_map/reduce_scatter | solution.py:88
  252.7 91.0 %collective-permute-start = (bf16[128,2,128]{2,1,0:T(2,128)(2,1)S(1)}, bf16[128,2,128]{2,1,0:T(2,128)(2,1)S(1)}, u32[]{:S(2)}, u32[]{:S(2)}) collective-permute-start(bf16[128,2,128]{2,1,0:T(2,128)(2,1)S(1)} %get-tuple-element.10), channel_id=1, source_target_pairs={{0,4},{4,8},{8,12},{12,16},{16,20},{20,24},{24,28},{28,32},{32,36}... | collective-permute-start | bytes 196616 | tf_op jit(solution)/shard_map/ppermute | solution.py:15
  254.7 94.6 %collective-permute-start.1 = (bf16[128,2,128]{2,1,0:T(2,128)(2,1)S(1)}, bf16[128,2,128]{2,1,0:T(2,128)(2,1)S(1)}, u32[]{:S(2)}, u32[]{:S(2)}) collective-permute-start(bf16[128,2,128]{2,1,0:T(2,128)(2,1)S(1)} %get-tuple-element.9), channel_id=1, source_target_pairs={{0,8},{4,12},{8,16},{12,20},{16,24},{20,28},{24,32},{28,36},{32,40... | collective-permute-start | bytes 196616 | tf_op jit(solution)/shard_map/ppermute | solution.py:15
  258.1 113.8 %collective-permute-start.2 = (bf16[128,2,128]{2,1,0:T(2,128)(2,1)S(1)}, bf16[128,2,128]{2,1,0:T(2,128)(2,1)S(1)}, u32[]{:S(2)}, u32[]{:S(2)}) collective-permute-start(bf16[128,2,128]{2,1,0:T(2,128)(2,1)S(1)} %get-tuple-element.8), channel_id=1, source_target_pairs={{0,12},{4,16},{8,20},{12,24},{16,28},{20,32},{24,36},{28,40},{32,4... | collective-permute-start | bytes 196616 | tf_op jit(solution)/shard_map/ppermute | solution.py:15
  262.3 109.7 %collective-permute-start.3 = (bf16[128,2,128]{2,1,0:T(2,128)(2,1)S(1)}, bf16[128,2,128]{2,1,0:T(2,128)(2,1)S(1)}, u32[]{:S(2)}, u32[]{:S(2)}) collective-permute-start(bf16[128,2,128]{2,1,0:T(2,128)(2,1)S(1)} %get-tuple-element.7), channel_id=1, source_target_pairs={{0,16},{4,20},{8,24},{12,28},{16,32},{20,36},{24,40},{28,44},{32,4... | collective-permute-start | bytes 196616 | tf_op jit(solution)/shard_map/ppermute | solution.py:15
  266.9 121.4 %collective-permute-start.4 = (bf16[128,2,128]{2,1,0:T(2,128)(2,1)S(1)}, bf16[128,2,128]{2,1,0:T(2,128)(2,1)S(1)}, u32[]{:S(2)}, u32[]{:S(2)}) collective-permute-start(bf16[128,2,128]{2,1,0:T(2,128)(2,1)S(1)} %get-tuple-element.6), channel_id=1, source_target_pairs={{0,20},{4,24},{8,28},{12,32},{16,36},{20,40},{24,44},{28,48},{32,5... | collective-permute-start | bytes 196616 | tf_op jit(solution)/shard_map/ppermute | solution.py:15
  343.7 45.3 %collective-permute-start.5 = (bf16[128,2,128]{2,1,0:T(2,128)(2,1)S(1)}, bf16[128,2,128]{2,1,0:T(2,128)(2,1)S(1)}, u32[]{:S(2)}, u32[]{:S(2)}) collective-permute-start(bf16[128,2,128]{2,1,0:T(2,128)(2,1)S(1)} %get-tuple-element.5), channel_id=1, source_target_pairs={{0,24},{4,28},{8,32},{12,36},{16,40},{20,44},{24,48},{28,52},{32,5... | collective-permute-start | bytes 196616 | tf_op jit(solution)/shard_map/ppermute | solution.py:15
  349.4 40.3 %collective-permute-start.6 = (bf16[128,2,128]{2,1,0:T(2,128)(2,1)S(1)}, bf16[128,2,128]{2,1,0:T(2,128)(2,1)}, u32[]{:S(2)}, u32[]{:S(2)}) collective-permute-start(bf16[128,2,128]{2,1,0:T(2,128)(2,1)S(1)} %get-tuple-element.4), channel_id=1, source_target_pairs={{0,28},{4,32},{8,36},{12,40},{16,44},{20,48},{24,52},{28,56},{32,6... | collective-permute-start | bytes 196616 | tf_op jit(solution)/shard_map/ppermute | solution.py:15
  372.1 0.8 copy-start.5
Sparse Core Ops, SparseCore 0:
  10.7 33.8 all-gather.2
  388.4 26.9 reduce-scatter.1
